TPU v7x, 32 devices: a whole 2x2x4 slice. The times are simulated.
32 devices in a mesh: kvh: 4 (over y, x), seq: 8 (over z, core).
Axes of the slice: x: 2, y: 2, z: 4, core: 2. Of those that a mesh axis runs over, the one named last changes fastest.
Arguments:
- queries: bfloat16 [4, 128, 128], P(None, 'kvh'), may hold values from -256 to 256
- keys: bfloat16 [4, 8, 1024, 128], P(None, 'kvh', 'seq'), may hold values from -6 to 6
- values: bfloat16 [4, 8, 1024, 128], P(None, 'kvh', 'seq'), may hold values from -6 to 6
- lengths: int32 [4, 8], P(None, 'seq'), may hold values from 2 to 128
- hidden_in: bfloat16 [4, 16384], P(None, ('kvh', 'seq')), may hold values from -10 to 10
- out_weight: bfloat16 [16384, 16384], P(('kvh', 'seq')), may hold values from -1 to 1
- norm_gain: bfloat16 [16384], replicated, may hold values from 0.3984375 to 1.59375
Outputs:
- attended: bfloat16 [4, 16384], P(None, ('kvh', 'seq'))
- normed: bfloat16 [4, 16384], P(None, ('kvh', 'seq'))
All inputs are finite; a program needn't handle non-finite values.
Results may differ from a plain program's by a relative error of at most 0.006.
Values may be sent and summed in bfloat16 or wider, within the bound.
A program may use at most 64 MiB of HBM per device.

v0:
```python
import jax
import jax.numpy as jnp
from jax import lax
from jax.sharding import PartitionSpec as P


def merged(shard, axis, combine):
    everything = jax.tree.map(lambda part: lax.all_gather(part, axis), shard)
    leading = jax.tree.map(lambda part: part[0], everything)

    def lap(k, so_far):
        return combine(so_far, jax.tree.map(lambda part: part[k], everything))

    return lax.fori_loop(1, lax.axis_size(axis), lap, leading)


def softmax_pair(first, second):
    highest = jnp.maximum(first[0], second[0])
    first_scale = jnp.exp(first[0] - highest)
    second_scale = jnp.exp(second[0] - highest)
    weight_total = first[1] * first_scale + second[1] * second_scale
    output_total = first[2] * first_scale[..., None] + second[2] * second_scale[..., None]
    return (highest, weight_total, output_total)


def body(queries, keys, values, lengths, hidden_in, out_weight, norm_gain):
    rows, heads_here, head_dim = queries.shape
    groups = keys.shape[1]
    positions = keys.shape[2]
    per_group = heads_here // groups
    query_grid = queries.reshape(rows, groups, per_group, head_dim)
    scores = jnp.einsum(
        "rkgd,rktd->rkgt", query_grid, keys, preferred_element_type=jnp.float32
    ) * head_dim ** (-0.5)
    valid = (jnp.arange(positions, dtype=jnp.int32)[None, :] < lengths)[:, None, None, :]
    peak_here = jnp.max(jnp.where(valid, scores, -jnp.inf), axis=-1)
    probs = jnp.exp(jnp.where(valid, scores - peak_here[..., None], -jnp.inf)).astype(jnp.bfloat16)
    weight_here = jnp.sum(probs, axis=-1, dtype=jnp.float32)
    partial_value = jnp.einsum("rkgt,rktd->rkgd", probs, values, preferred_element_type=jnp.float32)
    feature_width = heads_here * head_dim // lax.axis_size("seq")
    feature_start = lax.axis_index("seq") * feature_width
    highest, weight_total, output_total = merged(
        (peak_here, weight_here, partial_value), "seq", softmax_pair
    )
    whole_out = (output_total / weight_total[..., None]).reshape(rows, heads_here * head_dim)
    attention = lax.dynamic_slice_in_dim(whole_out, feature_start, feature_width, 1)
    attention = attention.astype(jnp.bfloat16)
    projected = jnp.dot(attention, out_weight, preferred_element_type=jnp.float32)
    slice_width = hidden_in.shape[1]
    slice_start = lax.axis_index(("kvh", "seq")) * slice_width
    gain_wide = norm_gain.astype(jnp.float32)
    projected_all = lax.psum(projected, ("kvh", "seq"))
    residual = lax.all_gather(hidden_in, ("kvh", "seq"), axis=1, tiled=True)
    stream_all = (residual.astype(jnp.float32) + projected_all).astype(jnp.bfloat16)
    stream_wide = stream_all.astype(jnp.float32)
    mean_square = jnp.mean(stream_wide * stream_wide, axis=1, keepdims=True)
    normed_all = (stream_wide * lax.rsqrt(mean_square + 1e-05) * gain_wide[None, :]).astype(
        jnp.bfloat16
    )
    attended = lax.dynamic_slice_in_dim(stream_all, slice_start, slice_width, 1)
    normed = lax.dynamic_slice_in_dim(normed_all, slice_start, slice_width, 1)
    return (attended, normed)


def solution(mesh):
    placed = (
        P(None, "kvh", None),
        P(None, "kvh", "seq", None),
        P(None, "kvh", "seq", None),
        P(None, "seq"),
        P(None, ("kvh", "seq")),
        P(("kvh", "seq"), None),
        P(),
    )
    return jax.shard_map(
        body,
        mesh=mesh,
        in_specs=placed,
        out_specs=(P(None, ("kvh", "seq")), P(None, ("kvh", "seq"))),
        check_vma=False,
    )
```

profile of v0, /device:TPU:0, one launch (start us, length us, event | category | flops | bytes accessed | tf_op | source)
XLA Modules:
  0.0 202.7 jit_solution(11224662813829926813)
XLA Ops:
  7.2 0.0 copy-start
  7.2 0.0 copy-start.1
  7.2 0.0 all-reduce.2.cloned.1.call-start
  7.2 0.8 iota_compare_fusion
  8.0 0.1 copy-done
  8.1 1.1 select_reduce_fusion
  9.2 15.8 %all-gather = f32[32,2,16]{2,1,0:T(2,128)S(1)} all-gather(f32[4,2,16]{2,1,0:T(2,128)S(1)} %get-tuple-element.201), channel_id=2, replica_groups=mesh['kvh'=4,'seq'=8] {'seq'}, dimensions={0}, use_global_device_ids=true | all-gather | bytes 4608 | tf_op jit(solution)/shard_map/all_gather | solution.py:8
  25.0 0.2 convert_reduce_fusion
  25.2 1.2 fusion.6
  26.4 14.8 %all-gather.2 = f32[32,2,16,128]{3,2,1,0:T(8,128)S(1)} all-gather(f32[4,2,16,128]{3,2,1,0:T(8,128)S(1)} %fusion.6), channel_id=4, replica_groups=mesh['kvh'=4,'seq'=8] {'seq'}, dimensions={0}, use_global_device_ids=true | all-gather | bytes 589824 | tf_op jit(solution)/shard_map/all_gather | solution.py:8
  41.2 14.2 %all-gather.1 = f32[32,2,16]{2,1,0:T(2,128)S(1)} all-gather(f32[4,2,16]{2,1,0:T(2,128)S(1)} %convert_reduce_fusion), channel_id=3, replica_groups=mesh['kvh'=4,'seq'=8] {'seq'}, dimensions={0}, use_global_device_ids=true | all-gather | bytes 4608 | tf_op jit(solution)/shard_map/all_gather | solution.py:8
  55.4 1.2 while.19
  55.4 0.1 fusion.17
  55.6 0.1 fusion.17
  55.7 0.1 fusion.17
  55.9 0.1 fusion.17
  56.1 0.1 fusion.17
  56.3 0.1 fusion.17
  56.4 0.1 fusion.17
  56.6 0.1 broadcast_divide_fusion
  56.7 8.8 %fusion.5 = f32[4,16384]{1,0:T(4,128)} fusion(bf16[512,16384]{1,0:T(8,128)(2,1)} %param.14, bf16[4,4096]{1,0:T(4,128)(2,1)S(1)} %bitcast.37, s32[]{:T(128)S(6)} %select_n.28), kind=kOutput, calls=%fused_computation.20 | convolution fusion | flops 67108864 | bytes 17043460 | tf_op jit(solution)/shard_map/dot_general | solution.py:48
  65.4 0.0 all-reduce.2.cloned.1.call-update
  65.5 0.8 dynamic-slice
  66.2 0.0 copy-done.1
  66.2 42.1 %all_gather.21 = bf16[4,16384]{1,0:T(4,128)(2,1)S(1)} all-gather(bf16[4,512]{1,0:T(4,128)(2,1)S(1)} %copy-done.1), channel_id=1, replica_groups=mesh['kvh'=4,'seq'=8] {'kvh','seq'}, dimensions={1}, use_global_device_ids=true | all-gather | bytes 135168 | tf_op jit(solution)/shard_map/all_gather | solution.py:53
  108.4 85.0 %all-reduce.2.cloned.1.call-done = f32[4,16384]{1,0:T(4,128)} async-done(((f32[4,16384]{1,0:T(4,128)}), f32[4,16384]{1,0:T(4,128)}) %all-reduce.2.cloned.1.call-update) | async-done | bytes 262160 | tf_op jit(solution)/shard_map/psum | solution.py:52
  193.4 1.2 multiply_reduce_fusion
  194.6 0.6 constant_dynamic-slice_fusion
  195.2 0.7 fusion.4
  (13 shorter events, 0.3 us)
Async XLA Ops:
  7.2 1.0 copy-start
  7.2 59.1 %copy-start.1 = (bf16[4,512]{1,0:T(4,128)(2,1)S(1)}, bf16[4,512]{1,0:T(4,128)(2,1)}, u32[]{:S(2)}) copy-start(bf16[4,512]{1,0:T(4,128)(2,1)} %param.13) | copy-start | bytes 12292
  7.2 186.2 %all-reduce.2.cloned.1.call-start = ((), (), s32[]{:S(2)}) async-start(), calls=%async_computation | async-start | bytes 524288 | tf_op jit(solution)/shard_map/psum | solution.py:52
Sparse Core Ops, SparseCore 0:
  65.6 127.7 all-reduce.1
where the time goes:
time: 203 us
  blocking collectives  86.9 us (43%)
  waiting for transfers between devices  85 us (42%)
  between operations  14.1 us (7%)
  matrix products  11 us (5%)
  other arithmetic  3.94 us (2%)
    psum x1, waiting for transfers between devices, body(): projected_all = lax.psum(projected, ('kvh', 'seq'))  85 us
    all_gather x3, blocking collectives, merged(): everything = jax.tree.map(lambda part: lax.all_gather(part, axis), shard)  44.8 us
    all_gather x1, blocking collectives, body(): residual = lax.all_gather(hidden_in, ('kvh', 'seq'), axis=1, tiled=True)  42.1 us
    dot_general x1, matrix products, body(): jnp.dot(attention, out_weight, preferred_element_type=jnp.float32)  8.75 us
  transfers between devices with their start and end apart: 1, of which 1 were waited for; matrix products, arithmetic and copies ran while one was open for 0% of the time, Pallas kernels for 0%

commit v1 on v0

--- a/solution.py
+++ b/solution.py
@@ -49,7 +49,7 @@
     slice_width = hidden_in.shape[1]
     slice_start = lax.axis_index(("kvh", "seq")) * slice_width
     gain_wide = norm_gain.astype(jnp.float32)
-    projected_all = lax.psum(projected, ("kvh", "seq"))
+    projected_all = jnp.sum(lax.all_gather(projected, ("kvh", "seq")), axis=0)
     residual = lax.all_gather(hidden_in, ("kvh", "seq"), axis=1, tiled=True)
     stream_all = (residual.astype(jnp.float32) + projected_all).astype(jnp.bfloat16)
     stream_wide = stream_all.astype(jnp.float32)

time: 203 us -> 157 us (0.77)
  waiting for transfers between devices: 85 us -> 35.2 us
  other arithmetic: 3.94 us -> 7.74 us
    psum x1 -> x0, waiting for transfers between devices: 85 us -> none  [body(): projected_all = lax.psum(projected, ('kvh', 'seq'))]
    all_gather x0 -> x1, waiting for transfers between devices: none -> 35.1 us  [body(): projected_all = jnp.sum(lax.all_gather(projected, ('kvh', 'seq')), axis=0)]
    reduce_sum x0 -> x1, other arithmetic: none -> 4.75 us  [body(): projected_all = jnp.sum(lax.all_gather(projected, ('kvh', 'seq')), axis=0)]
where the time goes in v1:
time: 157 us
  blocking collectives  87.3 us (56%)
  waiting for transfers between devices  35.2 us (22%)
  between operations  14.1 us (9%)
  matrix products  11 us (7%)
  other arithmetic  7.74 us (5%)
    all_gather x3, blocking collectives, merged(): everything = jax.tree.map(lambda part: lax.all_gather(part, axis), shard)  44.8 us
    all_gather x1, blocking collectives, body(): residual = lax.all_gather(hidden_in, ('kvh', 'seq'), axis=1, tiled=True)  42.5 us
    all_gather x1, waiting for transfers between devices, body(): projected_all = jnp.sum(lax.all_gather(projected, ('kvh', 'seq')), axis=0)  35.1 us
    dot_general x1, matrix products, body(): jnp.dot(attention, out_weight, preferred_element_type=jnp.float32)  8.76 us
    reduce_sum x1, other arithmetic, body(): projected_all = jnp.sum(lax.all_gather(projected, ('kvh', 'seq')), axis=0)  4.75 us
  transfers between devices with their start and end apart: 1, of which 1 were waited for; matrix products, arithmetic and copies ran while one was open for 0% of the time, Pallas kernels for 0%

profile of v1, /device:TPU:0, one launch (start us, length us, event | category | flops | bytes accessed | tf_op | source)
XLA Modules:
  0.0 157.1 jit_solution(4504486294759392138)
XLA Ops:
  7.2 0.0 copy-start
  7.2 0.0 copy-start.1
  7.2 0.0 all-gather.7.cloned.1.call-start
  7.2 0.8 iota_compare_fusion
  8.0 0.1 copy-done
  8.1 1.1 select_reduce_fusion
  9.2 15.8 %all-gather = f32[32,2,16]{2,1,0:T(2,128)S(1)} all-gather(f32[4,2,16]{2,1,0:T(2,128)S(1)} %get-tuple-element.201), channel_id=2, replica_groups=mesh['kvh'=4,'seq'=8] {'seq'}, dimensions={0}, use_global_device_ids=true | all-gather | bytes 4608 | tf_op jit(solution)/shard_map/all_gather | solution.py:8
  25.0 0.2 convert_reduce_fusion
  25.2 1.2 fusion.5
  26.4 14.8 %all-gather.2 = f32[32,2,16,128]{3,2,1,0:T(8,128)S(1)} all-gather(f32[4,2,16,128]{3,2,1,0:T(8,128)S(1)} %fusion.5), channel_id=4, replica_groups=mesh['kvh'=4,'seq'=8] {'seq'}, dimensions={0}, use_global_device_ids=true | all-gather | bytes 589824 | tf_op jit(solution)/shard_map/all_gather | solution.py:8
  41.2 14.2 %all-gather.1 = f32[32,2,16]{2,1,0:T(2,128)S(1)} all-gather(f32[4,2,16]{2,1,0:T(2,128)S(1)} %convert_reduce_fusion), channel_id=3, replica_groups=mesh['kvh'=4,'seq'=8] {'seq'}, dimensions={0}, use_global_device_ids=true | all-gather | bytes 4608 | tf_op jit(solution)/shard_map/all_gather | solution.py:8
  55.4 1.2 while.19
  55.4 0.1 fusion.16
  55.6 0.1 fusion.16
  55.7 0.1 fusion.16
  55.9 0.1 fusion.16
  56.1 0.1 fusion.16
  56.3 0.1 fusion.16
  56.4 0.1 fusion.16
  56.6 0.1 broadcast_divide_fusion
  56.7 8.8 %convolution_bitcast_fusion = f32[1,4,16384]{2,1,0:T(4,128)} fusion(bf16[512,16384]{1,0:T(8,128)(2,1)} %param.14, bf16[4,4096]{1,0:T(4,128)(2,1)S(1)} %bitcast.39, s32[]{:T(128)S(6)} %select_n.28), kind=kOutput, calls=%fused_computation.8 | convolution fusion | flops 67108864 | bytes 17043460 | tf_op jit(solution)/shard_map/dot_general | solution.py:48
  65.4 0.0 all-gather.7.cloned.1.call-update
  65.5 0.8 dynamic-slice
  66.2 0.0 copy-done.1
  66.2 42.5 %all_gather.27 = bf16[4,16384]{1,0:T(4,128)(2,1)S(1)} all-gather(bf16[4,512]{1,0:T(4,128)(2,1)S(1)} %copy-done.1), channel_id=1, replica_groups=mesh['kvh'=4,'seq'=8] {'kvh','seq'}, dimensions={1}, use_global_device_ids=true | all-gather | bytes 135168 | tf_op jit(solution)/shard_map/all_gather | solution.py:53
  108.8 35.1 %all-gather.7.cloned.1.call-done = f32[32,4,16384]{2,1,0:T(4,128)} async-done(((f32[1,4,16384]{2,1,0:T(4,128)}), f32[32,4,16384]{2,1,0:T(4,128)}) %all-gather.7.cloned.1.call-update) | async-done | bytes 8388624 | tf_op jit(solution)/shard_map/all_gather | solution.py:52
  143.9 4.8 %reduce_sum.28 = f32[4,16384]{1,0:T(4,128)S(1)} reduce(f32[32,4,16384]{2,1,0:T(4,128)} %all-gather.7.cloned.1.call-done, f32[]{:T(128)} %constant.56.clone.1), dimensions={0}, to_apply=%region_4.5 | reduce | flops 2031616 | bytes 8650756 | tf_op jit(solution)/shard_map/reduce_sum | solution.py:52
  148.7 0.3 multiply_reduce_fusion
  149.0 0.6 constant_dynamic-slice_fusion
  149.6 0.7 fusion.4
  (13 shorter events, 0.3 us)
Async XLA Ops:
  7.2 1.0 copy-start
  7.2 59.1 %copy-start.1 = (bf16[4,512]{1,0:T(4,128)(2,1)S(1)}, bf16[4,512]{1,0:T(4,128)(2,1)}, u32[]{:S(2)}) copy-start(bf16[4,512]{1,0:T(4,128)(2,1)} %param.13) | copy-start | bytes 12292
  7.2 136.7 %all-gather.7.cloned.1.call-start = ((), (), s32[]{:S(2)}) async-start(), calls=%async_computation | async-start | bytes 8650752 | tf_op jit(solution)/shard_map/all_gather | solution.py:52
Sparse Core Ops, SparseCore 0:
  65.6 78.2 all-gather.6

commit v2 on v0

--- a/solution.py
+++ b/solution.py
@@ -49,7 +49,7 @@
     slice_width = hidden_in.shape[1]
     slice_start = lax.axis_index(("kvh", "seq")) * slice_width
     gain_wide = norm_gain.astype(jnp.float32)
-    projected_all = lax.psum(projected, ("kvh", "seq"))
+    projected_all = lax.psum(lax.psum(projected, "kvh"), "seq")
     residual = lax.all_gather(hidden_in, ("kvh", "seq"), axis=1, tiled=True)
     stream_all = (residual.astype(jnp.float32) + projected_all).astype(jnp.bfloat16)
     stream_wide = stream_all.astype(jnp.float32)

time: 203 us -> 177 us (0.87)
  waiting for transfers between devices: 85 us -> 60.2 us
    psum x1 -> x2, waiting for transfers between devices: 85 us -> 60.2 us  [body(): projected_all = lax.psum(lax.psum(projected, 'kvh'), 'seq')]
  transfers between devices with their start and end apart: 1 -> 2, of which waited for: 1 -> 2; matrix products, arithmetic and copies ran while one was open for 0% -> 0% of each run, Pallas kernels for 0% -> 0%
where the time goes in v2:
time: 177 us
  blocking collectives  85.8 us (48%)
  waiting for transfers between devices  60.2 us (34%)
  between operations  14.1 us (8%)
  matrix products  11 us (6%)
  other arithmetic  3.94 us (2%)
    psum x2, waiting for transfers between devices, body(): projected_all = lax.psum(lax.psum(projected, 'kvh'), 'seq')  60.2 us
    all_gather x3, blocking collectives, merged(): everything = jax.tree.map(lambda part: lax.all_gather(part, axis), shard)  44.8 us
    all_gather x1, blocking collectives, body(): residual = lax.all_gather(hidden_in, ('kvh', 'seq'), axis=1, tiled=True)  41 us
    dot_general x1, matrix products, body(): jnp.dot(attention, out_weight, preferred_element_type=jnp.float32)  8.75 us
  transfers between devices with their start and end apart: 2, of which 2 were waited for; matrix products, arithmetic and copies ran while one was open for 0% of the time, Pallas kernels for 0%

profile of v2, /device:TPU:0, one launch (start us, length us, event | category | flops | bytes accessed | tf_op | source)
XLA Modules:
  0.0 176.9 jit_solution(7410875265733757859)
XLA Ops:
  7.2 0.0 copy-start
  7.2 0.0 copy-start.1
  7.2 0.0 all-reduce.3.cloned.1.call-start
  7.2 0.8 iota_compare_fusion
  8.0 0.1 copy-done
  8.1 1.1 select_reduce_fusion
  9.2 15.8 %all-gather = f32[32,2,16]{2,1,0:T(2,128)S(1)} all-gather(f32[4,2,16]{2,1,0:T(2,128)S(1)} %get-tuple-element.201), channel_id=2, replica_groups=mesh['kvh'=4,'seq'=8] {'seq'}, dimensions={0}, use_global_device_ids=true | all-gather | bytes 4608 | tf_op jit(solution)/shard_map/all_gather | solution.py:8
  25.0 0.2 convert_reduce_fusion
  25.2 1.2 fusion.6
  26.4 14.8 %all-gather.2 = f32[32,2,16,128]{3,2,1,0:T(8,128)S(1)} all-gather(f32[4,2,16,128]{3,2,1,0:T(8,128)S(1)} %fusion.6), channel_id=4, replica_groups=mesh['kvh'=4,'seq'=8] {'seq'}, dimensions={0}, use_global_device_ids=true | all-gather | bytes 589824 | tf_op jit(solution)/shard_map/all_gather | solution.py:8
  41.2 14.2 %all-gather.1 = f32[32,2,16]{2,1,0:T(2,128)S(1)} all-gather(f32[4,2,16]{2,1,0:T(2,128)S(1)} %convert_reduce_fusion), channel_id=3, replica_groups=mesh['kvh'=4,'seq'=8] {'seq'}, dimensions={0}, use_global_device_ids=true | all-gather | bytes 4608 | tf_op jit(solution)/shard_map/all_gather | solution.py:8
  55.4 1.2 while.19
  55.4 0.1 fusion.17
  55.6 0.1 fusion.17
  55.7 0.1 fusion.17
  55.9 0.1 fusion.17
  56.1 0.1 fusion.17
  56.3 0.1 fusion.17
  56.4 0.1 fusion.17
  56.6 0.1 broadcast_divide_fusion
  56.7 8.8 %fusion.5 = f32[4,16384]{1,0:T(4,128)} fusion(bf16[512,16384]{1,0:T(8,128)(2,1)} %param.14, bf16[4,4096]{1,0:T(4,128)(2,1)S(1)} %bitcast.37, s32[]{:T(128)S(6)} %select_n.28), kind=kOutput, calls=%fused_computation.20 | convolution fusion | flops 67108864 | bytes 17043460 | tf_op jit(solution)/shard_map/dot_general | solution.py:48
  65.4 0.0 all-reduce.3.cloned.1.call-update
  65.5 0.0 all-reduce.5.cloned.1.call-start
  65.5 44.2 %all-reduce.3.cloned.1.call-done = f32[4,16384]{1,0:T(4,128)} async-done(((f32[4,16384]{1,0:T(4,128)}), f32[4,16384]{1,0:T(4,128)}) %all-reduce.3.cloned.1.call-update) | async-done | bytes 262160 | tf_op jit(solution)/shard_map/psum | solution.py:52
  109.8 0.0 all-reduce.5.cloned.1.call-update
  109.8 0.8 dynamic-slice
  110.6 0.0 copy-done.1
  110.6 41.0 %all_gather.21 = bf16[4,16384]{1,0:T(4,128)(2,1)S(1)} all-gather(bf16[4,512]{1,0:T(4,128)(2,1)S(1)} %copy-done.1), channel_id=1, replica_groups=mesh['kvh'=4,'seq'=8] {'kvh','seq'}, dimensions={1}, use_global_device_ids=true | all-gather | bytes 135168 | tf_op jit(solution)/shard_map/all_gather | solution.py:53
  151.6 15.9 %all-reduce.5.cloned.1.call-done = f32[4,16384]{1,0:T(4,128)} async-done(((f32[4,16384]{1,0:T(4,128)}), f32[4,16384]{1,0:T(4,128)}) %all-reduce.5.cloned.1.call-update) | async-done | bytes 262160 | tf_op jit(solution)/shard_map/psum | solution.py:52
  167.5 1.2 multiply_reduce_fusion
  168.8 0.6 constant_dynamic-slice_fusion
  169.4 0.7 fusion.4
  (13 shorter events, 0.3 us)
Async XLA Ops:
  7.2 1.0 copy-start
  7.2 103.4 %copy-start.1 = (bf16[4,512]{1,0:T(4,128)(2,1)S(1)}, bf16[4,512]{1,0:T(4,128)(2,1)}, u32[]{:S(2)}) copy-start(bf16[4,512]{1,0:T(4,128)(2,1)} %param.13) | copy-start | bytes 12292
  7.2 102.6 %all-reduce.3.cloned.1.call-start = ((), (), s32[]{:S(2)}) async-start(), calls=%async_computation | async-start | bytes 524288 | tf_op jit(solution)/shard_map/psum | solution.py:52
  65.5 102.1 %all-reduce.5.cloned.1.call-start = ((), (), s32[]{:S(2)}) async-start(), calls=%async_computation.1 | async-start | bytes 524288 | tf_op jit(solution)/shard_map/psum | solution.py:52
Sparse Core Ops, SparseCore 0:
  65.6 44.1 all-reduce.2
  112.1 55.4 all-reduce.4
